TPU v7x, 256 devices: a whole 4x4x8 slice. The times are simulated.
256 devices in a mesh: slab: 64 (over z, x, core), view: 4 (over y).
Axes of the slice: x: 4, y: 4, z: 8, core: 2. Of those that a mesh axis runs over, the one named last changes fastest.
Arguments:
- activity: float32 [2048, 32, 1024], P('slab'), may hold values from 0.5 to 2
- sensitivity: float32 [2048, 32, 1024], P('slab'), may hold values from 1 to 8
- psf_width: float32 [2048], P('slab'), may hold values from 0.05 to 0.3
- measured: bfloat16 [4, 4096, 32, 128], P('view', 'slab'), may hold values from 0.25 to 4
- block_slab: int32 [4, 4096, 1], P('view', 'slab'), may hold values from 0 to 63; in each aligned block of 64 rows (0 to 63, 64 to 127, ..., all dimensions but the last counted through in order) at most 2 rows name the same one
- block_line: int32 [4, 4096], P('view', 'slab'), may hold values from 0 to 31
- block_angle: int32 [4, 4096], P('view', 'slab'), may hold values from 0 to 7
- subset_views: int32 [4, 8], P('view'), may hold values from 0 to 335
Outputs:
- updated: float32 [2048, 32, 1024], P('slab')
Inputs may be any that keep to these rules, and one draw needn't show every extreme that they name: `block_slab`: among the 64 blocks of one device (aligned blocks of 64 rows) no slab is named more than 2 times, a bound that some block reaches.
All inputs are finite; a program needn't handle non-finite values.
Results may differ from a plain program's by a relative error of at most 0.0014.
Values may be sent and summed in bfloat16 or wider, within the bound.
A program may use at most 64 MiB of HBM per device.

v0:
```python
import math
import jax
import jax.numpy as jnp
from jax import lax
from jax.sharding import PartitionSpec as P

VIEWS_ALL = 336
BACKGROUND = 0.05


def with_halo(value, sides, width):
    for axis, dim in sides:
        size, length = (lax.axis_size(axis), value.shape[dim])
        up = [(i, (i + 1) % size) for i in range(size - 1)]
        down = [(j, i) for i, j in up]
        last = lax.slice_in_dim(value, length - width, length, axis=dim)
        leading = lax.slice_in_dim(value, 0, width, axis=dim)
        before = lax.ppermute(last, axis, up)
        after = lax.ppermute(leading, axis, down)
        value = jnp.concatenate([before, value, after], axis=dim)
    return value


def kernels(angles, bins, length):
    view_angle = math.pi * angles.astype(jnp.float32) / VIEWS_ALL
    step_width = length / bins
    deviation = 0.25 * step_width
    spacing = step_width * (0.75 + 0.25 * jnp.cos(2.0 * view_angle))
    offset = 1.5 * step_width * jnp.sin(view_angle)
    centres = (jnp.arange(bins, dtype=jnp.float32) + 0.5 - bins / 2)[None, :] * spacing[
        :, None
    ] + offset[:, None]
    voxel_pos = jnp.arange(length, dtype=jnp.float32) + 0.5 - length / 2
    distance = voxel_pos[None, None, :] - centres[:, :, None]
    values = jnp.exp(-distance * distance / (2.0 * deviation * deviation)) / (
        deviation * math.sqrt(2.0 * math.pi)
    )
    return values.astype(jnp.bfloat16)


def on_device(
    activity, sensitivity, psf_width, measured, block_slab, block_line, block_angle, subset_views
):
    weight = psf_width[:, None, None]
    padded = with_halo(activity, (("slab", 0),), 1)
    blurred = ((1.0 - 2.0 * weight) * activity + weight * (padded[:-2] + padded[2:])).astype(
        jnp.bfloat16
    )
    planes, lines_here, length = activity.shape
    bins = measured.shape[3]
    tof_kernel = kernels(subset_views[0], bins, length)
    angle_count = tof_kernel.shape[0]
    projected = jnp.einsum("zlv,atv->alzt", blurred, tof_kernel, preferred_element_type=jnp.float32)
    projected = projected.reshape(angle_count * lines_here, planes, bins)
    slab_count = lax.axis_size("slab")
    block_total = measured.shape[1]
    capacity = 2 * block_total // slab_count
    targets = block_slab[0, :, 0]
    onehot = (targets[:, None] == jnp.arange(slab_count, dtype=jnp.int32)[None, :]).astype(
        jnp.int32
    )
    slot_pos = jnp.sum((jnp.cumsum(onehot, axis=0) - onehot) * onehot, axis=1)
    send_rows = (
        jnp.zeros((slab_count, capacity, planes, bins), jnp.bfloat16)
        .at[targets, slot_pos]
        .set(measured[0])
    )
    send_index = (
        jnp.zeros((slab_count, capacity), jnp.int32)
        .at[targets, slot_pos]
        .set(block_angle[0] * lines_here + block_line[0])
    )
    rows = lax.all_to_all(send_rows, "slab", split_axis=0, concat_axis=0, tiled=True)
    index = lax.all_to_all(send_index, "slab", split_axis=0, concat_axis=0, tiled=True)
    estimate = projected[index]
    ratios, index = (rows.astype(jnp.float32) / (estimate + BACKGROUND), index)
    sums = jnp.zeros((angle_count * lines_here, planes, bins), jnp.float32)
    sums = sums.at[index.reshape(-1)].add(ratios.reshape(-1, planes, bins))
    rounded = sums.astype(jnp.bfloat16).reshape(angle_count, lines_here, planes, bins)
    back = jnp.einsum("alzt,atv->zlv", rounded, tof_kernel, preferred_element_type=jnp.float32)
    total = lax.psum(back, "view")
    edges = with_halo(weight * total, (("slab", 0),), 1)
    smoothed = (1.0 - 2.0 * weight) * total + edges[:-2] + edges[2:]
    return activity * smoothed / sensitivity


def solution(mesh):
    in_specs = (
        P("slab", None, None),
        P("slab", None, None),
        P("slab"),
        P("view", "slab", None, None),
        P("view", "slab", None),
        P("view", "slab"),
        P("view", "slab"),
        P("view", None),
    )
    out_specs = P("slab", None, None)
    return jax.shard_map(
        on_device, mesh=mesh, in_specs=in_specs, out_specs=out_specs, check_vma=False
    )
```

profile of v0, /device:TPU:103, one launch (start us, length us, event | category | flops | bytes accessed | tf_op | source)
XLA Modules:
  0.0 249.0 jit_solution(8091599429287186392)
XLA Ops:
  6.5 0.7 fusion.23
  7.3 0.1 reduce_window_sum.11
  7.4 0.8 select_reduce_fusion
  8.2 0.7 fusion.26
  8.9 0.7 add_bitcast_fusion
  9.6 3.5 %scatter_fusion = s32[64,2]{0,1:T(2,128)S(1)} fusion(s32[64,2]{0,1:T(2,128)S(1)} %broadcast.188, s32[64]{0:T(128)S(1)} %fusion.26, s32[64]{0:T(128)S(1)} %add_bitcast_fusion), kind=kCustom, calls=%fused_computation.1 | custom fusion | bytes 1280 | tf_op jit(solution)/shard_map/scatter | solution.py:71
  13.1 0.7 copy.33
  13.8 11.0 %all-to-all-start = ((s32[64,1,2]{2,1,0:T(1,128)}), s32[64,1,2]{2,1,0:T(1,128)S(1)}, u32[]{:S(2)}, u32[]{:S(2)}) async-start(s32[64,1,2]{2,1,0:T(1,128)} %copy.33), calls=%async_computation | async-start | bytes 65536 | tf_op jit(solution)/shard_map/all_to_all | solution.py:74
  24.8 1.0 fusion.32
  25.8 0.1 copy.37
  25.9 2.3 collective-permute-start.1
  28.2 0.1 copy.35
  28.3 6.6 %collective-permute-start = (f32[1,32,1024]{2,0,1:T(1,128)S(1)}, f32[1,32,1024]{2,0,1:T(1,128)S(1)}, u32[]{:S(2)}, u32[]{:S(2)}) collective-permute-start(f32[1,32,1024]{2,0,1:T(1,128)S(1)} %copy.35), channel_id=1, source_target_pairs={{0,4},{4,8},{8,12},{12,16},{16,20},{20,24},{24,28},{28,32},{32,36}... | collective-permute-start | bytes 393224 | tf_op jit(solution)/shard_map/ppermute | solution.py:18
  35.0 0.7 multiply_bitcast_fusion
  35.7 0.1 multiply_add_fusion
  35.8 1.2 broadcast_in_dim.5
  37.0 8.0 %scatter_fusion.1 = bf16[64,2,32,128]{3,2,1,0:T(8,128)(2,1)} fusion(bf16[64,2,32,128]{3,2,1,0:T(8,128)(2,1)} %broadcast_in_dim.5, s32[64]{0:T(128)S(1)} %fusion.26, bf16[64,32,128]{2,1,0:T(8,128)(2,1)} %bitcast.57), kind=kCustom, calls=%fused_computation.2 | custom fusion | bytes 1573376 | tf_op jit(solution)/shard_map/scatter | solution.py:66
  45.0 8.6 %all-to-all-start.1 = ((bf16[64,2,32,128]{3,2,1,0:T(8,128)(2,1)}), bf16[64,2,32,128]{3,2,1,0:T(8,128)(2,1)S(1)}, u32[]{:S(2)}, u32[]{:S(2)}) async-start(bf16[64,2,32,128]{3,2,1,0:T(8,128)(2,1)} %scatter_fusion.1), calls=%async_computation.1 | async-start | bytes 2097152 | tf_op jit(solution)/shard_map/all_to_all | solution.py:73
  53.6 0.0 all-reduce.2.cloned.1.call-start
  53.7 6.6 %copy.44 = f32[32,32,1024]{2,0,1:T(8,128)} copy(f32[32,32,1024]{2,1,0:T(8,128)} %param.8) | data formatting | bytes 8388608 | tf_op args[0]
  60.3 0.6 broadcast.255
  60.9 0.8 reduce.3
  61.7 0.1 reshape.197
  61.8 0.1 copy.41
  61.9 0.1 copy.42
  62.0 0.2 reshape.207
  62.1 0.0 collective-permute-done.1
  62.2 0.0 collective-permute-done
  62.2 6.8 %fusion.11 = bf16[32,32,1024]{2,0,1:T(8,128)(2,1)S(1)} fusion(f32[1,32,1024]{2,0,1:T(1,128)S(1)} %collective-permute-done.1, f32[32,32,1024]{2,0,1:T(8,128)} %copy.44, f32[1,32,1024]{2,0,1:T(1,128)S(1)} %collective-permute-done, f32[32]{0:T(128)S(1)} %copy-done.2, f32[32]{0:T(128)S(1)} %multiply_subtract_fusion), kind=kLoop, calls=%fused_computation.19 | loop fusion | flops 7340032 | bytes 6553856 | tf_op jit(solution)/shard_map/convert_element_type | solution.py:46
  69.0 3.3 %convolution_bitcast_fusion.1 = f32[8,32,32,128]{3,1,2,0:T(8,128)S(1)} fusion(bf16[32,32,1024]{2,0,1:T(8,128)(2,1)S(1)} %fusion.11, f32[8,128]{1,0:T(8,128)S(1)} %multiply_add_fusion, f32[1024]{0:T(1024)S(1)} %iota_add_fusion), kind=kOutput, calls=%fused_computation.22 | convolution fusion | flops 2153775104 | bytes 6299648 | tf_op jit(solution)/shard_map/zlv,atv->alzt/dot_general | solution.py:53
  72.3 4.4 %copy.40 = f32[8,32,32,128]{3,2,1,0:T(8,128)} copy(f32[8,32,32,128]{3,1,2,0:T(8,128)S(1)} %convolution_bitcast_fusion.1) | data formatting | bytes 8388608 | tf_op jit(solution)/shard_map/zlv,atv->alzt/transpose | solution.py:53
  76.7 2.9 %gather_fusion = f32[128,32,128]{2,1,0:T(8,128)S(1)} fusion(f32[256,32,128]{2,1,0:T(8,128)} %bitcast.53, s32[1024]{0:T(1024)S(1)} %pad_clamp_fusion), kind=kCustom, calls=%fused_computation | custom fusion | bytes 4194816 | tf_op jit(solution)/shard_map/gather | solution.py:75
  79.5 1.6 broadcast_add_fusion
  81.1 0.0 all-to-all-done.1
  81.1 2.0 convert_divide_fusion
  83.1 2.5 %broadcast_in_dim.4 = f32[256,32,128]{2,1,0:T(8,128)} broadcast(f32[]{:T(128)} %constant.17.clone.1), dimensions={} | broadcast | bytes 4194308 | tf_op jit(solution)/shard_map/broadcast_in_dim | solution.py:77
  85.6 18.3 %scatter_fusion.2 = f32[256,32,128]{2,1,0:T(8,128)} fusion(f32[256,32,128]{2,1,0:T(8,128)} %broadcast_in_dim.4, s32[128]{0:T(128)S(1)} %fusion.25, f32[128,32,128]{2,1,0:T(8,128)S(1)} %bitcast.54), kind=kCustom, calls=%fused_computation.3 | custom fusion | flops 524288 | bytes 6291968 | tf_op jit(solution)/shard_map/scatter-add | solution.py:78
  103.9 2.7 %convert_element_type.31 = bf16[256,32,128]{2,1,0:T(8,128)(2,1)S(1)} convert(f32[256,32,128]{2,1,0:T(8,128)} %scatter_fusion.2) | non-fusion elementwise | flops 1048576 | bytes 6291456 | tf_op jit(solution)/shard_map/convert_element_type | solution.py:79
  106.6 4.6 %convolution_bitcast_fusion = f32[32,32,1024]{2,0,1:T(8,128)} fusion(bf16[8,32,32,128]{3,2,1,0:T(8,128)(2,1)S(1)} %bitcast.56, f32[8,128]{1,0:T(8,128)S(1)} %multiply_add_fusion, f32[1024]{0:T(1024)S(1)} %iota_add_fusion), kind=kOutput, calls=%fused_computation.21 | convolution fusion | flops 2153775104 | bytes 6299648 | tf_op jit(solution)/shard_map/alzt,atv->zlv/dot_general | solution.py:80
  111.2 0.0 all-reduce.2.cloned.1.call-update
  111.2 99.1 %all-reduce.2.cloned.1.call-done = f32[32,32,1024]{2,0,1:T(8,128)} async-done(((f32[32,32,1024]{2,0,1:T(8,128)}), f32[32,32,1024]{2,0,1:T(8,128)}) %all-reduce.2.cloned.1.call-update) | async-done | bytes 4194320 | tf_op jit(solution)/shard_map/psum | solution.py:81
  210.3 3.1 %broadcast_multiply_fusion = f32[32,32,1024]{2,0,1:T(8,128)S(1)} fusion(f32[32,32,1024]{2,0,1:T(8,128)} %all-reduce.2.cloned.1.call-done, f32[32]{0:T(128)S(1)} %copy-done.2), kind=kLoop, calls=%fused_computation.26 | loop fusion | flops 1048576 | bytes 8388736 | tf_op jit(solution)/shard_map/mul | solution.py:82
  213.4 0.2 fusion.31
  213.6 5.1 %collective-permute-start.2 = (f32[1,32,1024]{2,0,1:T(1,128)S(1)}, f32[1,32,1024]{2,0,1:T(1,128)S(1)}, u32[]{:S(2)}, u32[]{:S(2)}) collective-permute-start(f32[1,32,1024]{2,0,1:T(1,128)S(1)} %get-tuple-element.5), channel_id=1, source_target_pairs={{0,4},{4,8},{8,12},{12,16},{16,20},{20,24},{24,28},{28,32},{32,36}... | collective-permute-start | bytes 393224 | tf_op jit(solution)/shard_map/ppermute | solution.py:18
  218.7 1.9 collective-permute-start.3
  220.7 7.7 %collective-permute-done.3 = f32[1,32,1024]{2,0,1:T(1,128)S(1)} collective-permute-done((f32[1,32,1024]{2,0,1:T(1,128)S(1)}, f32[1,32,1024]{2,0,1:T(1,128)S(1)}, u32[]{:S(2)}, u32[]{:S(2)}) %collective-permute-start.3) | collective-permute-done | bytes 131104 | tf_op jit(solution)/shard_map/ppermute | solution.py:19
  228.3 9.4 %fusion.6 = f32[32,32,1024]{2,0,1:T(8,128)S(1)} fusion(f32[1,32,1024]{2,0,1:T(1,128)S(1)} %collective-permute-done.3, f32[32,32,1024]{2,0,1:T(8,128)S(1)} %broadcast_multiply_fusion, f32[1,32,1024]{2,0,1:T(1,128)S(1)} %collective-permute-done.2, f32[32,32,1024]{2,1,0:T(8,128)} %param.9, f32[32,32,1024]{2,0,1:T(8,128)S(1)} %copy-done.1, ...), kind=kLoop, calls=%fused_computation.12 | loop fusion | flops 7340032 | bytes 21233792 | tf_op jit(solution)/shard_map/div | solution.py:84
  237.7 4.4 %copy.46 = f32[32,32,1024]{2,1,0:T(8,128)} copy(f32[32,32,1024]{2,0,1:T(8,128)S(1)} %fusion.6) | data formatting | bytes 8388608 | tf_op jit(solution)/shard_map/div | solution.py:84
  (15 shorter events, 0.1 us)
Async XLA Ops:
  6.5 47.1 %copy-start.2 = (f32[32]{0:T(128)S(1)}, f32[32]{0:T(128)}, u32[]{:S(2)}) copy-start(f32[32]{0:T(128)} %param.10) | copy-start | bytes 388
  13.8 31.2 %all-to-all-start = ((s32[64,1,2]{2,1,0:T(1,128)}), s32[64,1,2]{2,1,0:T(1,128)S(1)}, u32[]{:S(2)}, u32[]{:S(2)}) async-start(s32[64,1,2]{2,1,0:T(1,128)} %copy.33), calls=%async_computation | async-start | bytes 65536 | tf_op jit(solution)/shard_map/all_to_all | solution.py:74
  25.9 36.2 %collective-permute-start.1 = (f32[1,32,1024]{2,0,1:T(1,128)S(1)}, f32[1,32,1024]{2,0,1:T(1,128)S(1)}, u32[]{:S(2)}, u32[]{:S(2)}) collective-permute-start(f32[1,32,1024]{2,0,1:T(1,128)S(1)} %copy.37), channel_id=1, source_target_pairs={{4,0},{8,4},{12,8},{16,12},{20,16},{24,20},{28,24},{32,28},{36,32}... | collective-permute-start | bytes 393224 | tf_op jit(solution)/shard_map/ppermute | solution.py:19
  28.3 33.8 %collective-permute-start = (f32[1,32,1024]{2,0,1:T(1,128)S(1)}, f32[1,32,1024]{2,0,1:T(1,128)S(1)}, u32[]{:S(2)}, u32[]{:S(2)}) collective-permute-start(f32[1,32,1024]{2,0,1:T(1,128)S(1)} %copy.35), channel_id=1, source_target_pairs={{0,4},{4,8},{8,12},{12,16},{16,20},{20,24},{24,28},{28,32},{32,36}... | collective-permute-start | bytes 393224 | tf_op jit(solution)/shard_map/ppermute | solution.py:18
  45.0 36.1 %all-to-all-start.1 = ((bf16[64,2,32,128]{3,2,1,0:T(8,128)(2,1)}), bf16[64,2,32,128]{3,2,1,0:T(8,128)(2,1)S(1)}, u32[]{:S(2)}, u32[]{:S(2)}) async-start(bf16[64,2,32,128]{3,2,1,0:T(8,128)(2,1)} %scatter_fusion.1), calls=%async_computation.1 | async-start | bytes 2097152 | tf_op jit(solution)/shard_map/all_to_all | solution.py:73
  53.6 156.8 %all-reduce.2.cloned.1.call-start = ((), (), s32[]{:S(2)}) async-start(), calls=%async_computation.2 | async-start | bytes 8388608 | tf_op jit(solution)/shard_map/psum | solution.py:81
  210.3 18.0 %copy-start = (f32[32,32,1024]{2,1,0:T(8,128)S(1)}, f32[32,32,1024]{2,1,0:T(8,128)}, u32[]{:S(2)}) copy-start(f32[32,32,1024]{2,1,0:T(8,128)} %param.8) | copy-start | bytes 12582916
  210.3 18.0 %copy-start.1 = (f32[32,32,1024]{2,0,1:T(8,128)S(1)}, f32[32,32,1024]{2,0,1:T(8,128)}, u32[]{:S(2)}) copy-start(f32[32,32,1024]{2,0,1:T(8,128)} %all-reduce.2.cloned.1.call-done) | copy-start | bytes 12582916
  213.6 7.0 %collective-permute-start.2 = (f32[1,32,1024]{2,0,1:T(1,128)S(1)}, f32[1,32,1024]{2,0,1:T(1,128)S(1)}, u32[]{:S(2)}, u32[]{:S(2)}) collective-permute-start(f32[1,32,1024]{2,0,1:T(1,128)S(1)} %get-tuple-element.5), channel_id=1, source_target_pairs={{0,4},{4,8},{8,12},{12,16},{16,20},{20,24},{24,28},{28,32},{32,36}... | collective-permute-start | bytes 393224 | tf_op jit(solution)/shard_map/ppermute | solution.py:18
  218.7 9.6 %collective-permute-start.3 = (f32[1,32,1024]{2,0,1:T(1,128)S(1)}, f32[1,32,1024]{2,0,1:T(1,128)S(1)}, u32[]{:S(2)}, u32[]{:S(2)}) collective-permute-start(f32[1,32,1024]{2,0,1:T(1,128)S(1)} %get-tuple-element.6), channel_id=1, source_target_pairs={{4,0},{8,4},{12,8},{16,12},{20,16},{24,20},{28,24},{32,28},{36,32}... | collective-permute-start | bytes 393224 | tf_op jit(solution)/shard_map/ppermute | solution.py:19
Sparse Core Ops, SparseCore 0:
  111.3 98.9 all-reduce.1
where the time goes:
time: 250 us; the launch traced here: 249 us
  waiting for transfers between devices  107 us (43%)
  other arithmetic  48.3 us (19%)
  local copies, waits for them, and re-layouts  36.9 us (15%)
  starting transfers between devices  35.5 us (14%)
  between operations  13.6 us (5%)
  matrix products  7.89 us (3%)
    psum x1, waiting for transfers between devices, on_device(): total = lax.psum(back, 'view')  99.1 us
    scatter-add x1, other arithmetic, on_device(): sums = sums.at[index.reshape(-1)].add(ratios.reshape(-1, planes, bins))  18.3 us
    ppermute x2, starting transfers between devices, with_halo(): before = lax.ppermute(last, axis, up)  11.7 us
    all_to_all x1, starting transfers between devices, on_device(): lax.all_to_all(send_index, 'slab', split_axis=0, concat_axis=0, tiled=True)  11 us
    div x1, other arithmetic, on_device(): return activity * smoothed / sensitivity  9.36 us
    all_to_all x1, starting transfers between devices, on_device(): lax.all_to_all(send_rows, 'slab', split_axis=0, concat_axis=0, tiled=True)  8.57 us
    scatter x1, local copies, waits for them, and re-layouts, on_device(): send_rows = jnp.zeros((slab_count, capacity, planes, bins), jnp.bfloat16)...  8 us
    ppermute x2, waiting for transfers between devices, with_halo(): after = lax.ppermute(leading, axis, down)  7.67 us
  transfers between devices with their start and end apart: 7, of which 2 were waited for; matrix products, arithmetic and copies ran while one was open for 16% of the time, Pallas kernels for 0%

commit v1 on v0

--- a/solution.py
+++ b/solution.py
@@ -78,7 +78,7 @@
     sums = sums.at[index.reshape(-1)].add(ratios.reshape(-1, planes, bins))
     rounded = sums.astype(jnp.bfloat16).reshape(angle_count, lines_here, planes, bins)
     back = jnp.einsum("alzt,atv->zlv", rounded, tof_kernel, preferred_element_type=jnp.float32)
-    total = lax.psum(back, "view")
+    total = jnp.sum(lax.all_gather(back, "view"), axis=0)
     edges = with_halo(weight * total, (("slab", 0),), 1)
     smoothed = (1.0 - 2.0 * weight) * total + edges[:-2] + edges[2:]
     return activity * smoothed / sensitivity

time: 250 us -> 318 us (1.27)
  waiting for transfers between devices: 107 us -> 165 us
  other arithmetic: 48.3 us -> 57.4 us
    all_gather x0 -> x1, waiting for transfers between devices: none -> 158 us  [on_device(): total = jnp.sum(lax.all_gather(back, 'view'), axis=0)]
    psum x1 -> x0, waiting for transfers between devices: 99.1 us -> none  [on_device(): total = lax.psum(back, 'view')]
    reduce_sum x0 -> x1, other arithmetic: none -> 10.4 us  [on_device(): total = jnp.sum(lax.all_gather(back, 'view'), axis=0)]
  transfers between devices with their start and end apart: 7 -> 7, of which waited for: 2 -> 2; matrix products, arithmetic and copies ran while one was open for 16% -> 12% of each run, Pallas kernels for 0% -> 0%
where the time goes in v1:
time: 318 us; the launch traced here: 317 us
  waiting for transfers between devices  165 us (52%)
  other arithmetic  57.4 us (18%)
  local copies, waits for them, and re-layouts  36.9 us (12%)
  starting transfers between devices  35.5 us (11%)
  between operations  13.6 us (4%)
  matrix products  7.87 us (2%)
    all_gather x1, waiting for transfers between devices, on_device(): total = jnp.sum(lax.all_gather(back, 'view'), axis=0)  158 us
    scatter-add x1, other arithmetic, on_device(): sums = sums.at[index.reshape(-1)].add(ratios.reshape(-1, planes, bins))  16.9 us
    ppermute x2, starting transfers between devices, with_halo(): before = lax.ppermute(last, axis, up)  11.7 us
    all_to_all x1, starting transfers between devices, on_device(): lax.all_to_all(send_index, 'slab', split_axis=0, concat_axis=0, tiled=True)  11 us
    reduce_sum x1, other arithmetic, on_device(): total = jnp.sum(lax.all_gather(back, 'view'), axis=0)  10.4 us
    div x1, other arithmetic, on_device(): return activity * smoothed / sensitivity  9.36 us
    all_to_all x1, starting transfers between devices, on_device(): lax.all_to_all(send_rows, 'slab', split_axis=0, concat_axis=0, tiled=True)  8.57 us
    scatter x1, local copies, waits for them, and re-layouts, on_device(): send_rows = jnp.zeros((slab_count, capacity, planes, bins), jnp.bfloat16)...  8 us
  transfers between devices with their start and end apart: 7, of which 2 were waited for; matrix products, arithmetic and copies ran while one was open for 12% of the time, Pallas kernels for 0%

profile of v1, /device:TPU:103, one launch (start us, length us, event | category | flops | bytes accessed | tf_op | source)
XLA Modules:
  0.0 316.5 jit_solution(8112238644249924897)
XLA Ops:
  6.5 0.7 fusion.23
  7.3 0.1 reduce_window_sum.11
  7.4 0.8 select_reduce_fusion
  8.2 0.7 fusion.26
  8.9 0.7 add_bitcast_fusion
  9.6 3.5 %scatter_fusion = s32[64,2]{0,1:T(2,128)S(1)} fusion(s32[64,2]{0,1:T(2,128)S(1)} %broadcast.188, s32[64]{0:T(128)S(1)} %fusion.26, s32[64]{0:T(128)S(1)} %add_bitcast_fusion), kind=kCustom, calls=%fused_computation.1 | custom fusion | bytes 1280 | tf_op jit(solution)/shard_map/scatter | solution.py:71
  13.1 0.7 copy.15
  13.8 11.0 %all-to-all-start = ((s32[64,1,2]{2,1,0:T(1,128)}), s32[64,1,2]{2,1,0:T(1,128)S(1)}, u32[]{:S(2)}, u32[]{:S(2)}) async-start(s32[64,1,2]{2,1,0:T(1,128)} %copy.15), calls=%async_computation | async-start | bytes 65536 | tf_op jit(solution)/shard_map/all_to_all | solution.py:74
  24.8 1.0 fusion.32
  25.8 0.1 copy.19
  25.9 2.3 collective-permute-start.1
  28.2 0.1 copy.17
  28.3 6.6 %collective-permute-start = (f32[1,32,1024]{2,0,1:T(1,128)S(1)}, f32[1,32,1024]{2,0,1:T(1,128)S(1)}, u32[]{:S(2)}, u32[]{:S(2)}) collective-permute-start(f32[1,32,1024]{2,0,1:T(1,128)S(1)} %copy.17), channel_id=1, source_target_pairs={{0,4},{4,8},{8,12},{12,16},{16,20},{20,24},{24,28},{28,32},{32,36}... | collective-permute-start | bytes 393224 | tf_op jit(solution)/shard_map/ppermute | solution.py:18
  35.0 0.7 multiply_bitcast_fusion
  35.7 0.1 multiply_add_fusion
  35.8 1.2 broadcast_in_dim.5
  37.0 8.0 %scatter_fusion.1 = bf16[64,2,32,128]{3,2,1,0:T(8,128)(2,1)} fusion(bf16[64,2,32,128]{3,2,1,0:T(8,128)(2,1)} %broadcast_in_dim.5, s32[64]{0:T(128)S(1)} %fusion.26, bf16[64,32,128]{2,1,0:T(8,128)(2,1)} %bitcast.59), kind=kCustom, calls=%fused_computation.2 | custom fusion | bytes 1573376 | tf_op jit(solution)/shard_map/scatter | solution.py:66
  45.0 8.6 %all-to-all-start.1 = ((bf16[64,2,32,128]{3,2,1,0:T(8,128)(2,1)}), bf16[64,2,32,128]{3,2,1,0:T(8,128)(2,1)S(1)}, u32[]{:S(2)}, u32[]{:S(2)}) async-start(bf16[64,2,32,128]{3,2,1,0:T(8,128)(2,1)} %scatter_fusion.1), calls=%async_computation.1 | async-start | bytes 2097152 | tf_op jit(solution)/shard_map/all_to_all | solution.py:73
  53.6 0.0 all-gather.3.cloned.1.call-start
  53.7 6.6 %copy.26 = f32[32,32,1024]{2,0,1:T(8,128)} copy(f32[32,32,1024]{2,1,0:T(8,128)} %param.8) | data formatting | bytes 8388608 | tf_op args[0]
  60.3 0.6 broadcast.255
  60.9 0.8 reduce.3
  61.7 0.1 reshape.197
  61.8 0.1 copy.23
  61.9 0.1 copy.24
  62.0 0.2 reshape.207
  62.1 0.0 collective-permute-done.1
  62.2 0.0 collective-permute-done
  62.2 6.8 %fusion.11 = bf16[32,32,1024]{2,0,1:T(8,128)(2,1)S(1)} fusion(f32[1,32,1024]{2,0,1:T(1,128)S(1)} %collective-permute-done.1, f32[32,32,1024]{2,0,1:T(8,128)} %copy.26, f32[1,32,1024]{2,0,1:T(1,128)S(1)} %collective-permute-done, f32[32]{0:T(128)S(1)} %copy-done.2, f32[32]{0:T(128)S(1)} %multiply_subtract_fusion), kind=kLoop, calls=%fused_computation.19 | loop fusion | flops 7340032 | bytes 6553856 | tf_op jit(solution)/shard_map/convert_element_type | solution.py:46
  69.0 3.3 %convolution_bitcast_fusion.1 = f32[8,32,32,128]{3,1,2,0:T(8,128)S(1)} fusion(bf16[32,32,1024]{2,0,1:T(8,128)(2,1)S(1)} %fusion.11, f32[8,128]{1,0:T(8,128)S(1)} %multiply_add_fusion, f32[1024]{0:T(1024)S(1)} %iota_add_fusion), kind=kOutput, calls=%fused_computation.22 | convolution fusion | flops 2153775104 | bytes 6299648 | tf_op jit(solution)/shard_map/zlv,atv->alzt/dot_general | solution.py:53
  72.3 4.4 %copy.22 = f32[8,32,32,128]{3,2,1,0:T(8,128)} copy(f32[8,32,32,128]{3,1,2,0:T(8,128)S(1)} %convolution_bitcast_fusion.1) | data formatting | bytes 8388608 | tf_op jit(solution)/shard_map/zlv,atv->alzt/transpose | solution.py:53
  76.7 2.9 gather_fusion
  79.6 1.6 broadcast_add_fusion
  81.1 2.0 convert_divide_fusion
  83.1 2.5 broadcast_in_dim.4
  85.7 16.9 %scatter_fusion.2 = f32[256,32,128]{2,1,0:T(8,128)} fusion(f32[256,32,128]{2,1,0:T(8,128)} %broadcast_in_dim.4, s32[128]{0:T(128)S(1)} %fusion.25, f32[128,32,128]{2,1,0:T(8,128)S(1)} %bitcast.56), kind=kCustom, calls=%fused_computation.3 | custom fusion | flops 524288 | bytes 6291968 | tf_op jit(solution)/shard_map/scatter-add | solution.py:78
  102.6 2.7 convert_element_type.31
  105.3 4.6 %convolution_bitcast_fusion = f32[32,32,1024]{2,0,1:T(8,128)} fusion(bf16[8,32,32,128]{3,2,1,0:T(8,128)(2,1)S(1)} %bitcast.58, f32[8,128]{1,0:T(8,128)S(1)} %multiply_add_fusion, f32[1024]{0:T(1024)S(1)} %iota_add_fusion), kind=kOutput, calls=%fused_computation.21 | convolution fusion | flops 2153775104 | bytes 6299648 | tf_op jit(solution)/shard_map/alzt,atv->zlv/dot_general | solution.py:80
  109.8 0.0 all-gather.3.cloned.1.call-update
  109.9 157.6 %all-gather.3.cloned.1.call-done = f32[128,32,1024]{2,0,1:T(8,128)} async-done(((f32[32,32,1024]{2,0,1:T(8,128)}), f32[128,32,1024]{2,0,1:T(8,128)}) %all-gather.3.cloned.1.call-update) | async-done | bytes 16777232 | tf_op jit(solution)/shard_map/all_gather | solution.py:81
  267.5 10.4 %reduce_sum.22 = f32[32,32,1024]{2,0,1:T(8,128)} reduce(f32[4,32,32,1024]{3,1,0,2:T(8,128)} %bitcast.54, f32[]{:T(128)} %constant.16.clone.1), dimensions={0}, to_apply=%region_5.6 | reduce | flops 3145728 | bytes 20971524 | tf_op jit(solution)/shard_map/reduce_sum | solution.py:81
  277.9 3.1 broadcast_multiply_fusion
  281.0 0.2 fusion.31
  281.2 5.1 %collective-permute-start.2 = (f32[1,32,1024]{2,0,1:T(1,128)S(1)}, f32[1,32,1024]{2,0,1:T(1,128)S(1)}, u32[]{:S(2)}, u32[]{:S(2)}) collective-permute-start(f32[1,32,1024]{2,0,1:T(1,128)S(1)} %get-tuple-element.5), channel_id=1, source_target_pairs={{0,4},{4,8},{8,12},{12,16},{16,20},{20,24},{24,28},{28,32},{32,36}... | collective-permute-start | bytes 393224 | tf_op jit(solution)/shard_map/ppermute | solution.py:18
  286.3 1.9 collective-permute-start.3
  288.2 7.7 %collective-permute-done.3 = f32[1,32,1024]{2,0,1:T(1,128)S(1)} collective-permute-done((f32[1,32,1024]{2,0,1:T(1,128)S(1)}, f32[1,32,1024]{2,0,1:T(1,128)S(1)}, u32[]{:S(2)}, u32[]{:S(2)}) %collective-permute-start.3) | collective-permute-done | bytes 131104 | tf_op jit(solution)/shard_map/ppermute | solution.py:19
  295.9 9.4 %fusion.6 = f32[32,32,1024]{2,0,1:T(8,128)S(1)} fusion(f32[1,32,1024]{2,0,1:T(1,128)S(1)} %collective-permute-done.3, f32[32,32,1024]{2,0,1:T(8,128)S(1)} %broadcast_multiply_fusion, f32[1,32,1024]{2,0,1:T(1,128)S(1)} %collective-permute-done.2, f32[32,32,1024]{2,1,0:T(8,128)} %param.9, f32[32,32,1024]{2,0,1:T(8,128)S(1)} %copy-done, ...), kind=kLoop, calls=%fused_computation.12 | loop fusion | flops 7340032 | bytes 21233792 | tf_op jit(solution)/shard_map/div | solution.py:84
  305.2 4.4 %copy.28 = f32[32,32,1024]{2,1,0:T(8,128)} copy(f32[32,32,1024]{2,0,1:T(8,128)S(1)} %fusion.6) | data formatting | bytes 8388608 | tf_op jit(solution)/shard_map/div | solution.py:84
  (16 shorter events, 0.1 us)
Async XLA Ops:
  6.5 47.1 %copy-start.2 = (f32[32]{0:T(128)S(1)}, f32[32]{0:T(128)}, u32[]{:S(2)}) copy-start(f32[32]{0:T(128)} %param.10) | copy-start | bytes 388
  13.8 31.2 %all-to-all-start = ((s32[64,1,2]{2,1,0:T(1,128)}), s32[64,1,2]{2,1,0:T(1,128)S(1)}, u32[]{:S(2)}, u32[]{:S(2)}) async-start(s32[64,1,2]{2,1,0:T(1,128)} %copy.15), calls=%async_computation | async-start | bytes 65536 | tf_op jit(solution)/shard_map/all_to_all | solution.py:74
  25.9 36.2 %collective-permute-start.1 = (f32[1,32,1024]{2,0,1:T(1,128)S(1)}, f32[1,32,1024]{2,0,1:T(1,128)S(1)}, u32[]{:S(2)}, u32[]{:S(2)}) collective-permute-start(f32[1,32,1024]{2,0,1:T(1,128)S(1)} %copy.19), channel_id=1, source_target_pairs={{4,0},{8,4},{12,8},{16,12},{20,16},{24,20},{28,24},{32,28},{36,32}... | collective-permute-start | bytes 393224 | tf_op jit(solution)/shard_map/ppermute | solution.py:19
  28.3 33.8 %collective-permute-start = (f32[1,32,1024]{2,0,1:T(1,128)S(1)}, f32[1,32,1024]{2,0,1:T(1,128)S(1)}, u32[]{:S(2)}, u32[]{:S(2)}) collective-permute-start(f32[1,32,1024]{2,0,1:T(1,128)S(1)} %copy.17), channel_id=1, source_target_pairs={{0,4},{4,8},{8,12},{12,16},{16,20},{20,24},{24,28},{28,32},{32,36}... | collective-permute-start | bytes 393224 | tf_op jit(solution)/shard_map/ppermute | solution.py:18
  45.0 36.1 %all-to-all-start.1 = ((bf16[64,2,32,128]{3,2,1,0:T(8,128)(2,1)}), bf16[64,2,32,128]{3,2,1,0:T(8,128)(2,1)S(1)}, u32[]{:S(2)}, u32[]{:S(2)}) async-start(bf16[64,2,32,128]{3,2,1,0:T(8,128)(2,1)} %scatter_fusion.1), calls=%async_computation.1 | async-start | bytes 2097152 | tf_op jit(solution)/shard_map/all_to_all | solution.py:73
  53.6 213.9 %all-gather.3.cloned.1.call-start = ((), (), s32[]{:S(2)}) async-start(), calls=%async_computation.2 | async-start | bytes 20971520 | tf_op jit(solution)/shard_map/all_gather | solution.py:81
  277.9 18.0 %copy-start = (f32[32,32,1024]{2,0,1:T(8,128)S(1)}, f32[32,32,1024]{2,0,1:T(8,128)}, u32[]{:S(2)}) copy-start(f32[32,32,1024]{2,0,1:T(8,128)} %reduce_sum.22) | copy-start | bytes 12582916
  277.9 18.0 %copy-start.1 = (f32[32,32,1024]{2,1,0:T(8,128)S(1)}, f32[32,32,1024]{2,1,0:T(8,128)}, u32[]{:S(2)}) copy-start(f32[32,32,1024]{2,1,0:T(8,128)} %param.8) | copy-start | bytes 12582916
  281.2 7.0 %collective-permute-start.2 = (f32[1,32,1024]{2,0,1:T(1,128)S(1)}, f32[1,32,1024]{2,0,1:T(1,128)S(1)}, u32[]{:S(2)}, u32[]{:S(2)}) collective-permute-start(f32[1,32,1024]{2,0,1:T(1,128)S(1)} %get-tuple-element.5), channel_id=1, source_target_pairs={{0,4},{4,8},{8,12},{12,16},{16,20},{20,24},{24,28},{28,32},{32,36}... | collective-permute-start | bytes 393224 | tf_op jit(solution)/shard_map/ppermute | solution.py:18
  286.3 9.6 %collective-permute-start.3 = (f32[1,32,1024]{2,0,1:T(1,128)S(1)}, f32[1,32,1024]{2,0,1:T(1,128)S(1)}, u32[]{:S(2)}, u32[]{:S(2)}) collective-permute-start(f32[1,32,1024]{2,0,1:T(1,128)S(1)} %get-tuple-element.6), channel_id=1, source_target_pairs={{4,0},{8,4},{12,8},{16,12},{20,16},{24,20},{28,24},{32,28},{36,32}... | collective-permute-start | bytes 393224 | tf_op jit(solution)/shard_map/ppermute | solution.py:19
Sparse Core Ops, SparseCore 0:
  110.0 157.4 all-gather.2
